TPU v7x, 32 devices: a whole 2x2x4 slice. The times are simulated.
32 devices in a mesh: dp: 8 (over z, y), tensor: 4 (over x, core).
Axes of the slice: x: 2, y: 2, z: 4, core: 2. Of those that a mesh axis runs over, the one named last changes fastest.
Arguments:
- tokens: bfloat16 [16, 2048, 768], P('dp', 'tensor'), may hold values from -6 to 6
- segment_ids: int32 [16, 2048], P('dp'), may hold values from 0 to 11, never falling along the last dimension, each value on 1 to 1024 neighbouring positions
- w_query: bfloat16 [768, 768], P('dp', 'tensor'), may hold values from -0.21875 to 0.21875
- w_key: bfloat16 [768, 768], P('dp', 'tensor'), may hold values from -0.21875 to 0.21875
- w_value: bfloat16 [768, 768], P('dp', 'tensor'), may hold values from -0.21875 to 0.21875
- w_out: bfloat16 [768, 768], P('tensor', 'dp'), may hold values from -1.25 to 1.25
- b_query: bfloat16 [12, 64], P('tensor', 'dp'), may hold values from -3 to 3
- b_value: bfloat16 [12, 64], P('tensor', 'dp'), may hold values from -3 to 3
- w_up: bfloat16 [768, 3072], P('dp', 'tensor'), may hold values from -0.21875 to 0.21875
- w_down: bfloat16 [3072, 768], P('tensor', 'dp'), may hold values from -0.109375 to 0.109375
- b_up: bfloat16 [48, 64], P('tensor', 'dp'), may hold values from -3 to 3
- b_out: bfloat16 [768], P(('dp', 'tensor')), may hold values from -3 to 3
- gain_one: bfloat16 [768], P(('dp', 'tensor')), may hold values from 0.25 to 1.75
- shift_one: bfloat16 [768], P(('dp', 'tensor')), may hold values from -3 to 3
- b_down: bfloat16 [768], P(('dp', 'tensor')), may hold values from -3 to 3
- gain_two: bfloat16 [768], P(('dp', 'tensor')), may hold values from 0.25 to 1.75
- shift_two: bfloat16 [768], P(('dp', 'tensor')), may hold values from -3 to 3
- cotangent: float32 [16, 2048, 768], P('dp', 'tensor'), may hold values from -6 to 6
Outputs:
- layer_out: float32 [16, 2048, 768], P('dp', 'tensor')
- grad_tokens: float32 [16, 2048, 768], P('dp', 'tensor')
- grad_w_query: float32 [768, 768], P('dp', 'tensor')
- grad_w_key: float32 [768, 768], P('dp', 'tensor')
- grad_w_value: float32 [768, 768], P('dp', 'tensor')
- grad_w_out: float32 [768, 768], P('tensor', 'dp')
- grad_b_query: float32 [12, 64], P('tensor', 'dp')
- grad_b_value: float32 [12, 64], P('tensor', 'dp')
- grad_w_up: float32 [768, 3072], P('dp', 'tensor')
- grad_w_down: float32 [3072, 768], P('tensor', 'dp')
- grad_b_up: float32 [48, 64], P('tensor', 'dp')
- grad_b_out: float32 [768], P(('dp', 'tensor'))
- grad_gain_one: float32 [768], P(('dp', 'tensor'))
- grad_shift_one: float32 [768], P(('dp', 'tensor'))
- grad_b_down: float32 [768], P(('dp', 'tensor'))
- grad_gain_two: float32 [768], P(('dp', 'tensor'))
- grad_shift_two: float32 [768], P(('dp', 'tensor'))
Inputs may be any that keep to these rules, and one draw needn't show every extreme that they name: `segment_ids`: in each sequence the segment numbers never fall and each of the 12 segments spans 1 to 1024 positions; some segment spans exactly 1024.
All inputs are finite; a program needn't handle non-finite values.
Results may differ from a plain program's by a relative error of at most 0.015.
Values may be sent and summed in bfloat16 or wider, within the bound.
No kernel may reach another device: no remote copies, remote signals or barrier semaphores. Data moves between devices by JAX's collectives and lax.ppermute only.
A program may use at most 192 MiB of HBM per device.

v0:
```python
import jax
import jax.numpy as jnp
from jax import lax
from jax.sharding import PartitionSpec as P

HD = 64
epsilon = 1e-12


def normalize(summed, gain, shift):
    centre = jnp.mean(summed, axis=-1, keepdims=True)
    centred = summed - centre
    spread = jnp.mean(centred * centred, axis=-1, keepdims=True)
    return centred * lax.rsqrt(spread + epsilon) * gain + shift


def gelu_exact(v):
    return jax.nn.gelu(v, approximate=False)


def block_scores(query_rows, key_heads, query_segs, key_segs, scale):
    scores = (
        jnp.einsum("qhd,khd->hqk", query_rows, key_heads, preferred_element_type=jnp.float32)
        * scale
    )
    same_doc = query_segs[:, None] == key_segs[None, :]
    return jnp.where(same_doc[None, :, :], scores, -1e30)


def attention_forward(queries, key_heads, value_heads, segments, block, scale):
    sequences, length = segments.shape
    blocks = length // block

    def one_block(index):
        which = index // blocks
        start = index % blocks * block
        query_rows = lax.dynamic_slice_in_dim(queries[which], start, block, 0)
        query_segs = lax.dynamic_slice_in_dim(segments[which], start, block, 0)
        scores = block_scores(query_rows, key_heads[which], query_segs, segments[which], scale)
        summit = jnp.max(scores, axis=-1, keepdims=True)
        raised = jnp.exp(scores - summit)
        totals = jnp.sum(raised, axis=-1, keepdims=True)
        weights = (raised / totals).astype(jnp.bfloat16)
        output = jnp.einsum(
            "hqk,khd->qhd", weights, value_heads[which], preferred_element_type=jnp.float32
        )
        return (output.astype(jnp.bfloat16), (summit + jnp.log(totals))[:, :, 0])

    outputs, logsums = lax.map(one_block, jnp.arange(sequences * blocks, dtype=jnp.int32))
    heads = queries.shape[2]
    context = outputs.reshape(sequences, length, heads, queries.shape[3])
    return (context, logsums.reshape(sequences, blocks, heads, block))


def attention_backward(
    queries, key_heads, value_heads, segments, logsums, grad_context, block, scale
):
    sequences, length = segments.shape
    blocks = length // block
    heads = queries.shape[2]
    head_size = queries.shape[3]

    def one_sequence(which):
        keys_here = key_heads[which]
        values_here = value_heads[which]
        segs_here = segments[which]

        def one_step(carry, position):
            gradient_key_rows, gradient_value_rows = carry
            start = position * block
            query_rows = lax.dynamic_slice_in_dim(queries[which], start, block, 0)
            grad_rows = lax.dynamic_slice_in_dim(grad_context[which], start, block, 0)
            query_segs = lax.dynamic_slice_in_dim(segs_here, start, block, 0)
            scores = block_scores(query_rows, keys_here, query_segs, segs_here, scale)
            weights = jnp.exp(scores - logsums[which, position][:, :, None])
            grad_weights = jnp.einsum(
                "qhd,khd->hqk", grad_rows, values_here, preferred_element_type=jnp.float32
            )
            inner_sum = jnp.sum(weights * grad_weights, axis=-1, keepdims=True)
            grad_scores = (weights * (grad_weights - inner_sum)).astype(jnp.bfloat16)
            grad_query = (
                jnp.einsum(
                    "hqk,khd->qhd", grad_scores, keys_here, preferred_element_type=jnp.float32
                )
                * scale
            )
            gradient_key_rows = (
                gradient_key_rows
                + jnp.einsum(
                    "hqk,qhd->khd", grad_scores, query_rows, preferred_element_type=jnp.float32
                )
                * scale
            )
            gradient_value_rows = gradient_value_rows + jnp.einsum(
                "hqk,qhd->khd",
                weights.astype(jnp.bfloat16),
                grad_rows,
                preferred_element_type=jnp.float32,
            )
            return ((gradient_key_rows, gradient_value_rows), grad_query.astype(jnp.bfloat16))

        zeros = jnp.zeros((length, heads, head_size), jnp.float32)
        (gradient_key_rows, gradient_value_rows), gradient_query_rows = lax.scan(
            one_step, (zeros, zeros), jnp.arange(blocks, dtype=jnp.int32)
        )
        return (
            gradient_query_rows.reshape(length, heads, head_size),
            gradient_key_rows.astype(jnp.bfloat16),
            gradient_value_rows.astype(jnp.bfloat16),
        )

    return lax.map(one_sequence, jnp.arange(sequences, dtype=jnp.int32))


def per_device(
    tokens,
    segment_ids,
    w_query,
    w_key,
    w_value,
    w_out,
    b_query,
    b_value,
    w_up,
    w_down,
    b_up,
    b_out,
    gain_one,
    shift_one,
    b_down,
    gain_two,
    shift_two,
    cotangent,
):
    (
        query_columns,
        key_columns,
        value_columns,
        output_rows,
        query_bias,
        value_bias,
        up_cols,
        down_rows,
        up_bias,
    ) = (
        lax.all_gather(w_query, "dp", axis=0, tiled=True),
        lax.all_gather(w_key, "dp", axis=0, tiled=True),
        lax.all_gather(w_value, "dp", axis=0, tiled=True),
        lax.all_gather(w_out, "dp", axis=1, tiled=True),
        lax.all_gather(b_query, "dp", axis=1, tiled=True),
        lax.all_gather(b_value, "dp", axis=1, tiled=True),
        lax.all_gather(w_up, "dp", axis=0, tiled=True),
        lax.all_gather(w_down, "dp", axis=1, tiled=True),
        lax.all_gather(b_up, "dp", axis=1, tiled=True),
    )
    vectors = (
        lax.all_gather(b_out, ("dp", "tensor"), axis=0, tiled=True),
        lax.all_gather(gain_one, ("dp", "tensor"), axis=0, tiled=True),
        lax.all_gather(shift_one, ("dp", "tensor"), axis=0, tiled=True),
        lax.all_gather(b_down, ("dp", "tensor"), axis=0, tiled=True),
        lax.all_gather(gain_two, ("dp", "tensor"), axis=0, tiled=True),
        lax.all_gather(shift_two, ("dp", "tensor"), axis=0, tiled=True),
    )
    out_bias, first_gain, first_shift, down_bias, second_gain, second_shift = [
        v.astype(jnp.float32) for v in vectors
    ]
    collected_rows = lax.all_gather(tokens, "tensor", axis=1, tiled=True)
    sequences, length, features = collected_rows.shape
    heads = query_columns.shape[1] // HD
    scale = HD ** (-0.5)
    block = min(512, length)

    def heads_of(weight_matrix, bias_vector):
        product = (
            jnp.einsum(
                "nfu,ua->nfa", collected_rows, weight_matrix, preferred_element_type=jnp.float32
            )
            + bias_vector
        )
        return product.astype(jnp.bfloat16).reshape(sequences, length, heads, HD)

    queries = heads_of(query_columns, query_bias.reshape(-1).astype(jnp.float32))
    key_heads = heads_of(key_columns, 0.0)
    value_heads = heads_of(value_columns, value_bias.reshape(-1).astype(jnp.float32))
    context, logsums = attention_forward(queries, key_heads, value_heads, segment_ids, block, scale)
    context_merged = context.reshape(sequences, length, heads * HD)
    partial_out = jnp.einsum(
        "zta,ag->ztg", context_merged, output_rows, preferred_element_type=jnp.float32
    )
    attended = lax.psum_scatter(partial_out, "tensor", scatter_dimension=1, tiled=True)
    summed = tokens.astype(jnp.float32) + attended + out_bias
    normed, first_pull = jax.vjp(normalize, summed, first_gain, first_shift)
    normed_low = normed.astype(jnp.bfloat16)
    normalized_total = lax.all_gather(normed_low, "tensor", axis=1, tiled=True)
    up_weight_used, down_weight_used, upbias_use = (up_cols, down_rows, up_bias)
    hidden_input = jnp.einsum(
        "uah,hg->uag", normalized_total, up_weight_used, preferred_element_type=jnp.float32
    )
    hidden_input = hidden_input + upbias_use.reshape(-1).astype(jnp.float32)
    activated, gelu_pull = jax.vjp(gelu_exact, hidden_input)
    activated_reduced = activated.astype(jnp.bfloat16)
    branch_part = jnp.einsum(
        "xvt,tw->xvw", activated_reduced, down_weight_used, preferred_element_type=jnp.float32
    )
    branch = lax.psum_scatter(branch_part, "tensor", scatter_dimension=1, tiled=True)
    layer_out, second_pull = jax.vjp(
        normalize, normed + branch + down_bias, second_gain, second_shift
    )
    grad_sum_two, grad_gain_two, grad_shift_two = second_pull(cotangent)
    grad_down_bias = jnp.sum(grad_sum_two, axis=(0, 1))
    grad_branch = grad_sum_two.astype(jnp.bfloat16)
    gradient_branch_total = lax.all_gather(grad_branch, "tensor", axis=1, tiled=True)
    grad_down = jnp.einsum(
        "ypw,ypv->wv", activated_reduced, gradient_branch_total, preferred_element_type=jnp.float32
    )
    grad_act = jnp.einsum(
        "mti,oi->mto", gradient_branch_total, down_weight_used, preferred_element_type=jnp.float32
    )
    gradient_hidden = gelu_pull(grad_act)[0].astype(jnp.bfloat16)
    grad_up_bias = jnp.sum(gradient_hidden, axis=(0, 1), dtype=jnp.float32).reshape(-1, HD)
    gradient_up_weight = jnp.einsum(
        "qwc,qwb->cb", normalized_total, gradient_hidden, preferred_element_type=jnp.float32
    )
    backward_portion = jnp.einsum(
        "hez,bz->heb", gradient_hidden, up_weight_used, preferred_element_type=jnp.float32
    )
    grad_normed = grad_sum_two + lax.psum_scatter(
        backward_portion, "tensor", scatter_dimension=1, tiled=True
    )
    grad_up_mine, grad_down_mine, grad_upbias_mine = (gradient_up_weight, grad_down, grad_up_bias)
    grad_summed, grad_gain_one, grad_shift_one = first_pull(grad_normed)
    grad_out_bias = jnp.sum(grad_summed, axis=(0, 1))
    gradient_rows_first = lax.all_gather(
        grad_summed.astype(jnp.bfloat16), "tensor", axis=1, tiled=True
    )
    grad_out_rows = jnp.einsum(
        "qwo,qwk->ok", context_merged, gradient_rows_first, preferred_element_type=jnp.float32
    )
    grad_context = jnp.einsum(
        "xpc,vc->xpv", gradient_rows_first, output_rows, preferred_element_type=jnp.float32
    )
    grad_context = grad_context.astype(jnp.bfloat16).reshape(sequences, length, heads, HD)
    gradient_query_rows, gradient_key_rows, gradient_value_rows = attention_backward(
        queries, key_heads, value_heads, segment_ids, logsums, grad_context, block, scale
    )
    flat_shape = (sequences, length, heads * HD)
    gradient_query_rows = gradient_query_rows.reshape(flat_shape)
    gradient_key_rows = gradient_key_rows.reshape(flat_shape)
    gradient_value_rows = gradient_value_rows.reshape(flat_shape)
    grad_query_cols = jnp.einsum(
        "hgb,hgu->bu", collected_rows, gradient_query_rows, preferred_element_type=jnp.float32
    )
    grad_key_cols = jnp.einsum(
        "hgb,hgu->bu", collected_rows, gradient_key_rows, preferred_element_type=jnp.float32
    )
    grad_value_cols = jnp.einsum(
        "hgb,hgu->bu", collected_rows, gradient_value_rows, preferred_element_type=jnp.float32
    )
    grad_query_bias = jnp.sum(gradient_query_rows, axis=(0, 1), dtype=jnp.float32).reshape(
        heads, HD
    )
    grad_value_bias = jnp.sum(gradient_value_rows, axis=(0, 1), dtype=jnp.float32).reshape(
        heads, HD
    )
    input_part = jnp.einsum(
        "vgr,hr->vgh", gradient_query_rows, query_columns, preferred_element_type=jnp.float32
    )
    input_part = input_part + jnp.einsum(
        "vgr,hr->vgh", gradient_key_rows, key_columns, preferred_element_type=jnp.float32
    )
    input_part = input_part + jnp.einsum(
        "vgr,hr->vgh", gradient_value_rows, value_columns, preferred_element_type=jnp.float32
    )
    grad_tokens = grad_summed + lax.psum_scatter(
        input_part.astype(jnp.bfloat16), "tensor", scatter_dimension=1, tiled=True
    ).astype(jnp.float32)
    weight_grads = (
        lax.psum_scatter(grad_query_cols, "dp", scatter_dimension=0, tiled=True),
        lax.psum_scatter(grad_key_cols, "dp", scatter_dimension=0, tiled=True),
        lax.psum_scatter(grad_value_cols, "dp", scatter_dimension=0, tiled=True),
        lax.psum_scatter(grad_out_rows, "dp", scatter_dimension=1, tiled=True),
        lax.psum_scatter(grad_query_bias, "dp", scatter_dimension=1, tiled=True),
        lax.psum_scatter(grad_value_bias, "dp", scatter_dimension=1, tiled=True),
        lax.psum_scatter(grad_up_mine, "dp", scatter_dimension=0, tiled=True),
        lax.psum_scatter(grad_down_mine, "dp", scatter_dimension=1, tiled=True),
        lax.psum_scatter(grad_upbias_mine, "dp", scatter_dimension=1, tiled=True),
    )
    vector_grads = (
        lax.psum_scatter(grad_out_bias, ("dp", "tensor"), scatter_dimension=0, tiled=True),
        lax.psum_scatter(grad_gain_one, ("dp", "tensor"), scatter_dimension=0, tiled=True),
        lax.psum_scatter(grad_shift_one, ("dp", "tensor"), scatter_dimension=0, tiled=True),
        lax.psum_scatter(grad_down_bias, ("dp", "tensor"), scatter_dimension=0, tiled=True),
        lax.psum_scatter(grad_gain_two, ("dp", "tensor"), scatter_dimension=0, tiled=True),
        lax.psum_scatter(grad_shift_two, ("dp", "tensor"), scatter_dimension=0, tiled=True),
    )
    return (
        layer_out,
        grad_tokens,
        weight_grads[0],
        weight_grads[1],
        weight_grads[2],
        weight_grads[3],
        weight_grads[4],
        weight_grads[5],
        weight_grads[6],
        weight_grads[7],
        weight_grads[8],
        vector_grads[0],
        vector_grads[1],
        vector_grads[2],
        vector_grads[3],
        vector_grads[4],
        vector_grads[5],
    )


def solution(mesh):
    in_specs = (
        P("dp", "tensor", None),
        P("dp", None),
        P("dp", "tensor"),
        P("dp", "tensor"),
        P("dp", "tensor"),
        P("tensor", "dp"),
        P("tensor", "dp"),
        P("tensor", "dp"),
        P("dp", "tensor"),
        P("tensor", "dp"),
        P("tensor", "dp"),
        P(("dp", "tensor")),
        P(("dp", "tensor")),
        P(("dp", "tensor")),
        P(("dp", "tensor")),
        P(("dp", "tensor")),
        P(("dp", "tensor")),
        P("dp", "tensor", None),
    )
    out_specs = (
        P("dp", "tensor", None),
        P("dp", "tensor", None),
        P("dp", "tensor"),
        P("dp", "tensor"),
        P("dp", "tensor"),
        P("tensor", "dp"),
        P("tensor", "dp"),
        P("tensor", "dp"),
        P("dp", "tensor"),
        P("tensor", "dp"),
        P("tensor", "dp"),
        P(("dp", "tensor")),
        P(("dp", "tensor")),
        P(("dp", "tensor")),
        P(("dp", "tensor")),
        P(("dp", "tensor")),
        P(("dp", "tensor")),
    )
    return jax.shard_map(
        per_device, mesh=mesh, in_specs=in_specs, out_specs=out_specs, check_vma=False
    )
```

profile of v0, /device:TPU:0, one launch (start us, length us, event | category | flops | bytes accessed | tf_op | source)
XLA Modules:
  0.0 1760.0 jit_solution(9406655017874332390)
XLA Ops:
  8.8 22.6 %all-gather.1 = bf16[8,8,3]{1,2,0:T(4,128)(2,1)S(1)} all-gather(bf16[1,8,3]{1,2,0:T(4,128)(2,1)} %bitcast.262), channel_id=1, replica_groups=mesh['dp'=8,'tensor'=4] {'dp'}, dimensions={0}, use_global_device_ids=true | all-gather | bytes 432 | tf_op jit(solution)/shard_map/all_gather | solution.py:150
  31.6 16.6 all-gather
  49.2 31.1 %all_gather.63 = bf16[192,768]{0,1:T(8,128)(2,1)S(1)} all-gather(bf16[192,96]{0,1:T(8,128)(2,1)S(1)} %copy.124), channel_id=1, replica_groups=mesh['dp'=8,'tensor'=4] {'dp'}, dimensions={1}, use_global_device_ids=true | all-gather | bytes 331776 | tf_op jit(solution)/shard_map/all_gather | solution.py:149
  80.4 31.2 %all_gather.60 = bf16[768,192]{1,0:T(8,128)(2,1)S(1)} all-gather(bf16[96,192]{1,0:T(8,128)(2,1)} %param.26), channel_id=1, replica_groups=mesh['dp'=8,'tensor'=4] {'dp'}, dimensions={0}, use_global_device_ids=true | all-gather | bytes 331776 | tf_op jit(solution)/shard_map/all_gather | solution.py:146
  111.5 31.4 %all_gather.62 = bf16[768,192]{1,0:T(8,128)(2,1)S(1)} all-gather(bf16[96,192]{1,0:T(8,128)(2,1)} %param.27), channel_id=1, replica_groups=mesh['dp'=8,'tensor'=4] {'dp'}, dimensions={0}, use_global_device_ids=true | all-gather | bytes 331776 | tf_op jit(solution)/shard_map/all_gather | solution.py:147
  142.9 31.2 %all_gather.58 = bf16[768,192]{1,0:T(8,128)(2,1)S(1)} all-gather(bf16[96,192]{1,0:T(8,128)(2,1)} %param.28), channel_id=1, replica_groups=mesh['dp'=8,'tensor'=4] {'dp'}, dimensions={0}, use_global_device_ids=true | all-gather | bytes 331776 | tf_op jit(solution)/shard_map/all_gather | solution.py:148
  187.4 225.8 %while.66 = (s32[]{:T(128)}, bf16[8,512,3,64]{1,3,2,0:T(8,128)(2,1)S(1)}, f32[8,3,512]{2,1,0:T(4,128)}, s32[8]{0:T(128)S(1)}, bf16[2,2048,3,64]{1,3,2,0:T(8,128)...) while((s32[]{:T(128)}, ...), condition=%wide.region_3.4_spmd, body=%wide.region_0.3_spmd.sunk | while | flops 844200448 | bytes 43995644 | solution.py:49
  193.3 8.4 fusion.133
  208.5 7.0 fusion.135
  221.4 8.4 fusion.133
  236.6 7.0 fusion.135
  249.6 8.4 fusion.133
  264.8 7.0 fusion.135
  277.7 8.4 fusion.133
  292.9 7.0 fusion.135
  305.9 8.4 fusion.133
  321.1 7.0 fusion.135
  334.0 8.4 fusion.133
  349.2 7.0 fusion.135
  362.2 8.4 fusion.133
  377.4 7.0 fusion.135
  390.4 8.4 fusion.133
  405.5 7.0 fusion.135
  426.1 39.3 %all-reduce.17 = (bf16[768]{0:T(1024)(128)(2,1)S(1)}, bf16[768]{0:T(1024)(128)(2,1)S(1)}, bf16[768]{0:T(1024)(128)(2,1)S(1)}, bf16[768]{0:T(1024)(128)(2,1)}, bf...) all-reduce(bf16[768]{0:T(1024)(128)(2,1)S(1)} %dynamic-update-slice, ...), channel_id=1, replica_groups=mesh['dp'=8,'tensor'=4] {'dp','tensor'}, use_global_device_ids=true, to_apply=%add | all-reduce | flops 4608 | bytes 18432
  465.4 57.9 %reduce-scatter.22.cloned.1.call-done = f32[2,512,768]{2,1,0:T(8,128)} async-done(((f32[2,2048,768]{2,1,0:T(8,128)}), f32[2,512,768]{2,1,0:T(8,128)}) %reduce-scatter.22.cloned.1.call-update) | async-done | bytes 3145744 | tf_op jit(solution)/shard_map/reduce_scatter | solution.py:190
  529.6 27.0 %all_gather.69 = bf16[12,64]{0,1:T(8,128)(2,1)} all-gather(bf16[12,8]{0,1:T(8,128)(2,1)} %param.34), channel_id=1, replica_groups=mesh['dp'=8,'tensor'=4] {'dp'}, dimensions={1}, use_global_device_ids=true | all-gather | bytes 1728 | tf_op jit(solution)/shard_map/all_gather | solution.py:154
  559.3 16.0 all-gather.11.cloned.1.call-done
  575.3 13.5 fusion.55
  593.2 31.8 %multiply_convert_fusion.1 = (bf16[2,2048,768]{2,1,0:T(8,128)(2,1)}, f32[2,2048,768]{2,1,0:T(8,128)}) fusion(f32[2,2048,768]{2,1,0:T(8,128)S(1)} %get-tuple-element.838, f32[768]{0:T(1024)S(1)} %copy-done.31, u8[2048,768]{1,0:T(8,128)(4,1)} %get-tuple-element.728, u8[2048,768]{1,0:T(8,128)(4,1)} %get-tuple-element.727), kind=kLoop, calls=%fused_computation.72 | loop fusion | flops 223346688 | bytes 34606080 | tf_op jit(solution)/shard_map/convert_element_type | solution.py:201
  625.1 10.2 fusion.65
  639.2 95.7 %reduce-scatter.24.cloned.1.call-done = f32[2,512,768]{2,1,0:T(8,128)} async-done(((f32[2,2048,768]{2,1,0:T(8,128)}), f32[2,512,768]{2,1,0:T(8,128)}) %reduce-scatter.24.cloned.1.call-update) | async-done | bytes 3145744 | tf_op jit(solution)/shard_map/reduce_scatter | solution.py:205
  747.4 46.5 %all-gather.17.cloned.1.call-done = bf16[2,2048,768]{2,1,0:T(8,128)(2,1)} async-done(((bf16[2,512,768]{2,1,0:T(8,128)(2,1)}), bf16[2,2048,768]{2,1,0:T(8,128)(2,1)}) %all-gather.17.cloned.1.call-update) | async-done | bytes 6291472 | tf_op jit(solution)/shard_map/all_gather | solution.py:212
  793.9 17.3 convert_reduce_fusion
  811.2 10.6 fusion.67
  821.9 99.8 %reduce-scatter.26.cloned.1.call-done = f32[2,512,768]{2,1,0:T(8,128)} async-done(((f32[2,2048,768]{2,1,0:T(8,128)}), f32[2,512,768]{2,1,0:T(8,128)}) %reduce-scatter.26.cloned.1.call-update) | async-done | bytes 3145744 | tf_op jit(solution)/shard_map/reduce_scatter | solution.py:227
  930.9 46.4 %all-gather.19.cloned.1.call-done = bf16[2,2048,768]{2,1,0:T(8,128)(2,1)} async-done(((bf16[2,512,768]{2,1,0:T(8,128)(2,1)}), bf16[2,2048,768]{2,1,0:T(8,128)(2,1)}) %all-gather.19.cloned.1.call-update) | async-done | bytes 6291472 | tf_op jit(solution)/shard_map/all_gather | solution.py:233
  990.5 326.1 %while.68 = (s32[]{:T(128)}, bf16[2,2048,3,64]{3,2,1,0:T(4,128)(2,1)}, bf16[2,2048,3,64]{1,3,2,0:T(8,128)(2,1)}, bf16[2,2048,3,64]{1,3,2,0:T(8,128)(2,1)}, s32[2...) while((s32[]{:T(128)}, ...), condition=%wide.region_19.20_spmd, body=%wide.region_15.19_spmd.sunk | while | flops 2064448000 | bytes 176434160 | solution.py:112
  997.9 144.7 %while.69 = (s32[]{:T(128)}, f32[2048,3,64]{0,2,1:T(8,128)}, f32[2048,3,64]{0,2,1:T(8,128)}, bf16[4,512,3,64]{1,3,2,0:T(8,128)(2,1)}, s32[4]{0:T(128)S(1)}, /*in...) while((s32[]{:T(128)}, f32[2048,3,64]{0,2,1:T(8,128)}, ...), condition=%wide.region_18.18_spmd.clone, body=%wide.region_16.17_spmd.clone.sunk | while | flops 2063661568 | bytes 143911376 | solution.py:103
  1160.8 144.7 %while.69 = (s32[]{:T(128)}, f32[2048,3,64]{0,2,1:T(8,128)}, f32[2048,3,64]{0,2,1:T(8,128)}, bf16[4,512,3,64]{1,3,2,0:T(8,128)(2,1)}, s32[4]{0:T(128)S(1)}, /*in...) while((s32[]{:T(128)}, f32[2048,3,64]{0,2,1:T(8,128)}, ...), condition=%wide.region_18.18_spmd.clone, body=%wide.region_16.17_spmd.clone.sunk | while | flops 2063661568 | bytes 143911376 | solution.py:103
  1335.0 12.1 add_convert_fusion
  1347.1 10.1 convolution_bitcast_fusion.1
  1357.3 10.9 convolution_bitcast_fusion
  1383.8 41.3 %all-reduce.15 = (f32[768]{0:T(1024)S(1)}, f32[768]{0:T(1024)S(1)}, f32[768]{0:T(1024)S(1)}, f32[768]{0:T(1024)S(1)}, f32[768]{0:T(1024)S(1)}, /*index=5*/f32[768]{0:T(1024)S(1)}) all-reduce(f32[768]{0:T(1024)S(1)} %copy-done.36, f32[768]{0:T(1024)S(1)} %copy-done.29, ...), channel_id=15, replica_groups=mesh['dp'=8,'tensor'=4] {'dp','tensor'}, use_global_device_ids=true, to_apply=%region_34.35.clone | all-reduce | flops 4608 | bytes 36864
  1443.7 37.5 %all-reduce.16 = (f32[3,64]{1,0:T(4,128)S(1)}, f32[3,64]{1,0:T(4,128)S(1)}, f32[12,64]{1,0:T(8,128)S(1)}) all-reduce(f32[3,64]{1,0:T(4,128)S(1)} %convert_reduce_fusion.1, f32[3,64]{1,0:T(4,128)S(1)} %convert_reduce_fusion.2, f32[12,64]{1,0:T(8,128)S(1)} %reshape.284), channel_id=10, replica_groups=mesh['dp'=8,'tensor'=4] {'dp'}, use_global_device_ids=true, to_apply=%region_26.27.clone | all-reduce | flops 1152 | bytes 9216
  1487.7 66.1 %reduce-scatter.32.cloned.1.call-done = f32[768,96]{0,1:T(8,128)} async-done(((f32[768,768]{0,1:T(8,128)}), f32[768,96]{0,1:T(8,128)}) %reduce-scatter.32.cloned.1.call-update) | async-done | bytes 294928 | tf_op jit(solution)/shard_map/reduce_scatter | solution.py:285
  1553.7 66.4 %reduce-scatter.34.cloned.1.call-done = f32[96,192]{1,0:T(8,128)} async-done(((f32[768,192]{1,0:T(8,128)}), f32[96,192]{1,0:T(8,128)}) %reduce-scatter.34.cloned.1.call-update) | async-done | bytes 73744
  1620.1 66.1 %reduce-scatter.36.cloned.1.call-done = f32[96,192]{1,0:T(8,128)} async-done(((f32[768,192]{1,0:T(8,128)}), f32[96,192]{1,0:T(8,128)}) %reduce-scatter.36.cloned.1.call-update) | async-done | bytes 73744
  1686.2 66.2 %reduce-scatter.38.cloned.1.call-done = f32[96,192]{1,0:T(8,128)} async-done(((f32[768,192]{1,0:T(8,128)}), f32[96,192]{1,0:T(8,128)}) %reduce-scatter.38.cloned.1.call-update) | async-done | bytes 73744
  (427 shorter events, 520.1 us)
Async XLA Ops:
  8.0 166.1 %all-gather.9.cloned.1.call-start = ((), (), s32[]{:S(2)}) async-start(), calls=%async_computation.10 | async-start | bytes 7864320 | tf_op jit(solution)/shard_map/all_gather | solution.py:167
  8.8 514.6 %reduce-scatter.22.cloned.1.call-start = ((), (), s32[]{:S(2)}) async-start(), calls=%async_computation.11 | async-start | bytes 15728640 | tf_op jit(solution)/shard_map/reduce_scatter | solution.py:190
  111.5 72.4 %copy-start.22 = (bf16[768,192]{1,0:T(8,128)(2,1)}, bf16[768,192]{1,0:T(8,128)(2,1)S(1)}, u32[]{:S(2)}) copy-start(bf16[768,192]{1,0:T(8,128)(2,1)S(1)} %all_gather.60) | copy-start | bytes 884740
  142.9 41.0 %copy-start.16 = (bf16[768,192]{1,0:T(8,128)(2,1)}, bf16[768,192]{1,0:T(8,128)(2,1)S(1)}, u32[]{:S(2)}) copy-start(bf16[768,192]{1,0:T(8,128)(2,1)S(1)} %all_gather.62) | copy-start | bytes 884740
  174.1 9.8 copy-start.18
  417.2 6.8 copy-start.13
  424.1 135.2 %all-gather.13.cloned.1.call-start = ((), (), s32[]{:S(2)}) async-start(), calls=%async_computation.13 | async-start | bytes 1327104 | tf_op jit(solution)/shard_map/all_gather | solution.py:152
  424.7 150.6 %all-gather.11.cloned.1.call-start = ((), (), s32[]{:S(2)}) async-start(), calls=%async_computation.12 | async-start | bytes 7864320 | tf_op jit(solution)/shard_map/all_gather | solution.py:194
  529.0 96.1 %all-gather.15.cloned.1.call-start = ((), (), s32[]{:S(2)}) async-start(), calls=%async_computation.14 | async-start | bytes 1327104 | tf_op jit(solution)/shard_map/all_gather | solution.py:153
  529.5 205.4 %reduce-scatter.24.cloned.1.call-start = ((), (), s32[]{:S(2)}) async-start(), calls=%async_computation.15 | async-start | bytes 15728640 | tf_op jit(solution)/shard_map/reduce_scatter | solution.py:205
  575.3 17.9 %copy-start.31 = (f32[768]{0:T(1024)S(1)}, f32[768]{0:T(1024)}, u32[]{:S(2)}) copy-start(f32[768]{0:T(1024)} %reshape.287) | copy-start | bytes 9220
  635.3 158.5 %all-gather.17.cloned.1.call-start = ((), (), s32[]{:S(2)}) async-start(), calls=%async_computation.16 | async-start | bytes 7864320 | tf_op jit(solution)/shard_map/all_gather | solution.py:212
  747.3 174.3 %reduce-scatter.26.cloned.1.call-start = ((), (), s32[]{:S(2)}) async-start(), calls=%async_computation.17 | async-start | bytes 15728640 | tf_op jit(solution)/shard_map/reduce_scatter | solution.py:227
  793.8 17.3 copy-start.38
  821.8 155.5 %all-gather.19.cloned.1.call-start = ((), (), s32[]{:S(2)}) async-start(), calls=%async_computation.18 | async-start | bytes 7864320 | tf_op jit(solution)/shard_map/all_gather | solution.py:233
  927.1 50.2 %copy-start.14 = (bf16[2,2048,192]{1,0,2:T(2,128)(2,1)S(1)}, bf16[2,2048,192]{1,0,2:T(2,128)(2,1)}, u32[]{:S(2)}) copy-start(bf16[2,2048,192]{1,0,2:T(2,128)(2,1)} %copy-done.13) | copy-start | bytes 4718596
  927.1 56.6 %copy-start.24 = (f32[2,512]{1,0:T(2,128)}, f32[2,512]{1,0:T(2,128)S(1)}, u32[]{:S(2)}) copy-start(f32[2,512]{1,0:T(2,128)S(1)} %negate_multiply_fusion.1) | copy-start | bytes 12292
  930.9 551.7 %reduce-scatter.40.cloned.1.call-start = ((), (), s32[]{:S(2)}) async-start(), calls=%async_computation.25 | async-start | bytes 884736
  983.8 500.4 %reduce-scatter.28.cloned.1.call-start = ((), (), s32[]{:S(2)}) async-start(), calls=%async_computation.19 | async-start | bytes 7864320 | tf_op jit(solution)/shard_map/reduce_scatter | solution.py:274
  990.5 331.7 %copy-start.17 = (bf16[768,192]{1,0:T(8,128)(2,1)S(1)}, bf16[768,192]{1,0:T(8,128)(2,1)}, u32[]{:S(2)}) copy-start(bf16[768,192]{1,0:T(8,128)(2,1)} %copy-done.16) | copy-start | bytes 884740
  997.9 7.9 copy-start.2
  1033.3 7.9 copy-start.2
  1069.8 7.9 copy-start.2
  1106.3 7.8 copy-start.2
  1142.7 7.2 copy-start.4
  1142.7 7.2 copy-start.10
  1160.8 7.9 copy-start.2
  1196.2 7.9 copy-start.2
  1232.7 7.9 copy-start.2
  1269.2 7.8 copy-start.2
  1305.5 7.2 copy-start.4
  1305.5 7.2 copy-start.10
  1322.2 6.4 copy-start.23
  1328.6 6.4 copy-start.19
  1347.1 140.6 %reduce-scatter.30.cloned.1.call-start = ((), (), s32[]{:S(2)}) async-start(), calls=%async_computation.20 | async-start | bytes 2654208 | tf_op jit(solution)/shard_map/reduce_scatter | solution.py:284
  1357.2 196.5 %reduce-scatter.32.cloned.1.call-start = ((), (), s32[]{:S(2)}) async-start(), calls=%async_computation.21 | async-start | bytes 2654208 | tf_op jit(solution)/shard_map/reduce_scatter | solution.py:285
  1368.2 252.0 %reduce-scatter.34.cloned.1.call-start = ((), (), s32[]{:S(2)}) async-start(), calls=%async_computation.22 | async-start | bytes 884736
  1376.2 7.6 copy-start.37
  1376.2 7.6 copy-start.29
  1376.2 7.6 copy-start.30
  1376.2 7.6 copy-start.33
  1376.2 7.6 copy-start.34
  1376.2 7.6 copy-start.35
  1376.2 7.6 copy-start.36
  1376.2 310.0 %reduce-scatter.36.cloned.1.call-start = ((), (), s32[]{:S(2)}) async-start(), calls=%async_computation.23 | async-start | bytes 884736
  1382.4 370.1 %reduce-scatter.38.cloned.1.call-start = ((), (), s32[]{:S(2)}) async-start(), calls=%async_computation.24 | async-start | bytes 884736
  1433.8 50.4 %copy-start.6 = (f32[2,512,768]{2,1,0:T(8,128)S(1)}, f32[2,512,768]{2,1,0:T(8,128)}, u32[]{:S(2)}) copy-start(f32[2,512,768]{2,1,0:T(8,128)} %copy-done.5) | copy-start | bytes 9437188
  1433.8 50.4 %copy-start.25 = (f32[2,512]{1,0:T(2,128)S(1)}, f32[2,512]{1,0:T(2,128)}, u32[]{:S(2)}) copy-start(f32[2,512]{1,0:T(2,128)} %copy-done.24) | copy-start | bytes 12292
  (45 other events, 162.6 us)
Sparse Core Ops, SparseCore 0:
  10.4 49.0 all-gather.8
  424.2 99.0 reduce-scatter.21
  747.4 46.3 all-gather.16
  931.0 46.3 all-gather.18
Sparse Core Ops, SparseCore 1:
  426.7 40.1 all-gather.12
  529.0 46.2 all-gather.10
  577.3 41.4 all-gather.14
  635.4 99.5 reduce-scatter.23
  821.9 99.7 reduce-scatter.25
  983.9 63.3 reduce-scatter.39
  1347.2 59.4 reduce-scatter.27
  1410.6 69.9 reduce-scatter.29
  1484.5 69.1 reduce-scatter.31
  1557.6 62.5 reduce-scatter.33
  1623.9 62.3 reduce-scatter.35
  1690.1 62.3 reduce-scatter.37
where the time goes:
time: 1770 us; the launch traced here: 1760 us
  waiting for transfers between devices  629 us (36%)
  matrix products  471 us (27%)
  blocking collectives  309 us (17%)
  other arithmetic  193 us (11%)
  local copies, waits for them, and re-layouts  92.6 us (5%)
  loops' own time  47.2 us (3%)
    unnamed x20, waiting for transfers between devices  201 us
    unnamed x3, blocking collectives  118 us
    reduce_scatter x1, waiting for transfers between devices, per_device(): lax.psum_scatter(backward_portion, 'tensor', scatter_dimension=1, tiled=T...  99.8 us
    reduce_scatter x1, waiting for transfers between devices, per_device(): lax.psum_scatter(branch_part, 'tensor', scatter_dimension=1, tiled=True)  95.7 us
    dot_general x16, matrix products, block_scores(): jnp.einsum('qhd,khd->hqk', query_rows, key_heads, preferred_element_type=...  92.9 us
    reduce_scatter x1, waiting for transfers between devices, per_device(): lax.psum_scatter(grad_down_mine, 'dp', scatter_dimension=1, tiled=True)  66.1 us
    reduce_scatter x1, waiting for transfers between devices, per_device(): lax.psum_scatter(partial_out, 'tensor', scatter_dimension=1, tiled=True)  57.9 us
    dot_general x8, matrix products, one_block(): jnp.einsum('hqk,khd->qhd', weights, value_heads[which], preferred_element...  55.7 us
  transfers between devices with their start and end apart: 16, of which 10 were waited for; matrix products, arithmetic and copies ran while one was open for 26% of the time, Pallas kernels for 0%

commit v1 on v0

--- a/solution.py
+++ b/solution.py
@@ -209,7 +209,23 @@
     grad_sum_two, grad_gain_two, grad_shift_two = second_pull(cotangent)
     grad_down_bias = jnp.sum(grad_sum_two, axis=(0, 1))
     grad_branch = grad_sum_two.astype(jnp.bfloat16)
-    gradient_branch_total = lax.all_gather(grad_branch, "tensor", axis=1, tiled=True)
+    ways, here, hop = (lax.axis_size("tensor"), lax.axis_index("tensor"), grad_branch.shape[1])
+    shape = [n * ways if d == 1 else n for d, n in enumerate(grad_branch.shape)]
+    full = lax.dynamic_update_slice_in_dim(
+        jnp.zeros(shape, grad_branch.dtype), grad_branch, here * hop, axis=1
+    )
+    going_up = going_down = grad_branch
+    for far in range(1, ways // 2 + 1):
+        going_up = lax.ppermute(going_up, "tensor", [(d, (d + 1) % ways) for d in range(ways)])
+        full = lax.dynamic_update_slice_in_dim(full, going_up, (here - far) % ways * hop, axis=1)
+        if 2 * far < ways:
+            going_down = lax.ppermute(
+                going_down, "tensor", [(d, (d - 1) % ways) for d in range(ways)]
+            )
+            full = lax.dynamic_update_slice_in_dim(
+                full, going_down, (here + far) % ways * hop, axis=1
+            )
+    gradient_branch_total = full
     grad_down = jnp.einsum(
         "ypw,ypv->wv", activated_reduced, gradient_branch_total, preferred_element_type=jnp.float32
     )

time: 1770 us -> 1790 us (1.011)
  local copies, waits for them, and re-layouts: 92.6 us -> 116 us
    all_gather x1 -> x0, waiting for transfers between devices: 46.5 us -> none  [per_device(): lax.all_gather(grad_branch, 'tensor', axis=1, tiled=True)]
    ppermute x0 -> x3, waiting for transfers between devices: none -> 36.8 us  [the longest x2 36.8 us: per_device(): lax.ppermute(going_up, 'tensor', [(d, (d + 1) % ways) for d in range(ways)])]
    unnamed x20 -> x19, waiting for transfers between devices: 201 us -> 201 us
  transfers between devices with their start and end apart: 16 -> 18, of which waited for: 10 -> 11; matrix products, arithmetic and copies ran while one was open for 26% -> 27% of each run, Pallas kernels for 0% -> 0%
where the time goes in v1:
time: 1790 us; the launch traced here: 1780 us
  waiting for transfers between devices  619 us (35%)
  matrix products  472 us (26%)
  blocking collectives  309 us (17%)
  other arithmetic  194 us (11%)
  local copies, waits for them, and re-layouts  116 us (6%)
  loops' own time  47.2 us (3%)
    unnamed x19, waiting for transfers between devices  201 us
    unnamed x3, blocking collectives  118 us
    reduce_scatter x1, waiting for transfers between devices, per_device(): lax.psum_scatter(backward_portion, 'tensor', scatter_dimension=1, tiled=T...  99.7 us
    reduce_scatter x1, waiting for transfers between devices, per_device(): lax.psum_scatter(branch_part, 'tensor', scatter_dimension=1, tiled=True)  95.9 us
    dot_general x16, matrix products, block_scores(): jnp.einsum('qhd,khd->hqk', query_rows, key_heads, preferred_element_type=...  92.8 us
    reduce_scatter x1, waiting for transfers between devices, per_device(): lax.psum_scatter(grad_down_mine, 'dp', scatter_dimension=1, tiled=True)  65.3 us
    reduce_scatter x1, waiting for transfers between devices, per_device(): lax.psum_scatter(partial_out, 'tensor', scatter_dimension=1, tiled=True)  57.9 us
    dot_general x8, matrix products, one_block(): jnp.einsum('hqk,khd->qhd', weights, value_heads[which], preferred_element...  55.7 us
  transfers between devices with their start and end apart: 18, of which 11 were waited for; matrix products, arithmetic and copies ran while one was open for 27% of the time, Pallas kernels for 0%

profile of v1, /device:TPU:0, one launch (start us, length us, event | category | flops | bytes accessed | tf_op | source)
XLA Modules:
  0.0 1775.5 jit_solution(11489797882300970648)
XLA Ops:
  8.8 22.6 %all-gather.1 = bf16[8,8,3]{1,2,0:T(4,128)(2,1)S(1)} all-gather(bf16[1,8,3]{1,2,0:T(4,128)(2,1)} %bitcast.262), channel_id=1, replica_groups=mesh['dp'=8,'tensor'=4] {'dp'}, dimensions={0}, use_global_device_ids=true | all-gather | bytes 432 | tf_op jit(solution)/shard_map/all_gather | solution.py:150
  31.6 16.6 all-gather
  49.2 31.1 %all_gather.60 = bf16[192,768]{0,1:T(8,128)(2,1)S(1)} all-gather(bf16[192,96]{0,1:T(8,128)(2,1)S(1)} %copy.140), channel_id=1, replica_groups=mesh['dp'=8,'tensor'=4] {'dp'}, dimensions={1}, use_global_device_ids=true | all-gather | bytes 331776 | tf_op jit(solution)/shard_map/all_gather | solution.py:149
  80.4 31.2 %all_gather.57 = bf16[768,192]{1,0:T(8,128)(2,1)S(1)} all-gather(bf16[96,192]{1,0:T(8,128)(2,1)} %param.26), channel_id=1, replica_groups=mesh['dp'=8,'tensor'=4] {'dp'}, dimensions={0}, use_global_device_ids=true | all-gather | bytes 331776 | tf_op jit(solution)/shard_map/all_gather | solution.py:146
  111.5 31.4 %all_gather.59 = bf16[768,192]{1,0:T(8,128)(2,1)S(1)} all-gather(bf16[96,192]{1,0:T(8,128)(2,1)} %param.27), channel_id=1, replica_groups=mesh['dp'=8,'tensor'=4] {'dp'}, dimensions={0}, use_global_device_ids=true | all-gather | bytes 331776 | tf_op jit(solution)/shard_map/all_gather | solution.py:147
  142.9 31.2 %all_gather.55 = bf16[768,192]{1,0:T(8,128)(2,1)S(1)} all-gather(bf16[96,192]{1,0:T(8,128)(2,1)} %param.28), channel_id=1, replica_groups=mesh['dp'=8,'tensor'=4] {'dp'}, dimensions={0}, use_global_device_ids=true | all-gather | bytes 331776 | tf_op jit(solution)/shard_map/all_gather | solution.py:148
  187.3 225.7 %while.66 = (s32[]{:T(128)}, bf16[8,512,3,64]{1,3,2,0:T(8,128)(2,1)S(1)}, f32[8,3,512]{2,1,0:T(4,128)}, s32[8]{0:T(128)S(1)}, bf16[2,2048,3,64]{1,3,2,0:T(8,128)...) while((s32[]{:T(128)}, ...), condition=%wide.region_3.4_spmd, body=%wide.region_0.3_spmd.sunk | while | flops 844200448 | bytes 43995644 | solution.py:49
  193.2 8.4 fusion.133
  208.4 7.0 fusion.135
  221.4 8.4 fusion.133
  236.6 7.0 fusion.135
  249.5 8.4 fusion.133
  264.7 7.0 fusion.135
  277.7 8.4 fusion.133
  292.8 7.0 fusion.135
  305.8 8.4 fusion.133
  321.0 7.0 fusion.135
  334.0 8.4 fusion.133
  349.1 7.0 fusion.135
  362.1 8.4 fusion.133
  377.3 7.0 fusion.135
  390.3 8.4 fusion.133
  405.4 7.0 fusion.135
  426.1 39.3 %all-reduce.17 = (bf16[768]{0:T(1024)(128)(2,1)S(1)}, bf16[768]{0:T(1024)(128)(2,1)S(1)}, bf16[768]{0:T(1024)(128)(2,1)S(1)}, bf16[768]{0:T(1024)(128)(2,1)}, bf...) all-reduce(bf16[768]{0:T(1024)(128)(2,1)S(1)} %dynamic-update-slice, ...), channel_id=1, replica_groups=mesh['dp'=8,'tensor'=4] {'dp','tensor'}, use_global_device_ids=true, to_apply=%add | all-reduce | flops 4608 | bytes 18432
  465.3 57.9 %reduce-scatter.22.cloned.1.call-done = f32[2,512,768]{2,1,0:T(8,128)} async-done(((f32[2,2048,768]{2,1,0:T(8,128)}), f32[2,512,768]{2,1,0:T(8,128)}) %reduce-scatter.22.cloned.1.call-update) | async-done | bytes 3145744 | tf_op jit(solution)/shard_map/reduce_scatter | solution.py:190
  529.5 27.0 %all_gather.66 = bf16[12,64]{0,1:T(8,128)(2,1)} all-gather(bf16[12,8]{0,1:T(8,128)(2,1)} %param.34), channel_id=1, replica_groups=mesh['dp'=8,'tensor'=4] {'dp'}, dimensions={1}, use_global_device_ids=true | all-gather | bytes 1728 | tf_op jit(solution)/shard_map/all_gather | solution.py:154
  559.2 16.0 all-gather.10.cloned.1.call-done
  575.2 13.5 fusion.55
  593.1 31.8 %multiply_convert_fusion.1 = (bf16[2,2048,768]{2,1,0:T(8,128)(2,1)}, f32[2,2048,768]{2,1,0:T(8,128)}) fusion(f32[2,2048,768]{2,1,0:T(8,128)S(1)} %get-tuple-element.838, f32[768]{0:T(1024)S(1)} %copy-done.32, u8[2048,768]{1,0:T(8,128)(4,1)} %get-tuple-element.728, u8[2048,768]{1,0:T(8,128)(4,1)} %get-tuple-element.727), kind=kLoop, calls=%fused_computation.72 | loop fusion | flops 223346688 | bytes 34606080 | tf_op jit(solution)/shard_map/convert_element_type | solution.py:201
  625.0 10.2 fusion.65
  639.1 95.9 %reduce-scatter.24.cloned.1.call-done = f32[2,512,768]{2,1,0:T(8,128)} async-done(((f32[2,2048,768]{2,1,0:T(8,128)}), f32[2,512,768]{2,1,0:T(8,128)}) %reduce-scatter.24.cloned.1.call-update) | async-done | bytes 3145744 | tf_op jit(solution)/shard_map/reduce_scatter | solution.py:205
  749.2 34.6 %collective-permute-done = bf16[2,512,768]{2,1,0:T(8,128)(2,1)} collective-permute-done((bf16[2,512,768]{2,1,0:T(8,128)(2,1)}, bf16[2,512,768]{2,1,0:T(8,128)(2,1)}, u32[]{:S(2)}, u32[]{:S(2)}) %collective-permute-start) | collective-permute-done | bytes 1572896 | tf_op jit(solution)/shard_map/ppermute | solution.py:219
  809.3 18.0 %convert_reduce_fusion = (f32[768]{0:T(1024)}, bf16[2,2048,768]{2,1,0:T(8,128)(2,1)}) fusion(f32[2,2048,768]{2,1,0:T(8,128)} %get-tuple-element.824, bf16[2,2048,768]{1,2,0:T(8,128)(2,1)} %constant_dynamic-update-slice_fusion, bf16[768,768]{0,1:T(8,128)(2,1)} %all-gather.14.cloned.1.call-done, f32[2,2048,768]{2,1,0:T(8,128)} %copy-done.8, f32[768]{0:T(1024)} %reshape.287), kind=kOutput, calls=%fused_computation.69 | convolution fusion | flops 4885314560 | bytes 38934528 | tf_op jit(solution)/shard_map/mti,oi->mto/dot_general | solution.py:232
  827.3 10.6 fusion.67
  838.0 99.7 %reduce-scatter.26.cloned.1.call-done = f32[2,512,768]{2,1,0:T(8,128)} async-done(((f32[2,2048,768]{2,1,0:T(8,128)}), f32[2,512,768]{2,1,0:T(8,128)}) %reduce-scatter.26.cloned.1.call-update) | async-done | bytes 3145744 | tf_op jit(solution)/shard_map/reduce_scatter | solution.py:243
  947.1 46.3 %all-gather.16.cloned.1.call-done = bf16[2,2048,768]{2,1,0:T(8,128)(2,1)} async-done(((bf16[2,512,768]{2,1,0:T(8,128)(2,1)}), bf16[2,2048,768]{2,1,0:T(8,128)(2,1)}) %all-gather.16.cloned.1.call-update) | async-done | bytes 6291472 | tf_op jit(solution)/shard_map/all_gather | solution.py:249
  1006.5 325.8 %while.68 = (s32[]{:T(128)}, bf16[2,2048,3,64]{3,2,1,0:T(4,128)(2,1)}, bf16[2,2048,3,64]{1,3,2,0:T(8,128)(2,1)}, bf16[2,2048,3,64]{1,3,2,0:T(8,128)(2,1)}, s32[2...) while((s32[]{:T(128)}, ...), condition=%wide.region_19.20_spmd, body=%wide.region_15.19_spmd.sunk | while | flops 2064448000 | bytes 176434160 | solution.py:112
  1013.9 144.6 %while.69 = (s32[]{:T(128)}, f32[2048,3,64]{0,2,1:T(8,128)}, f32[2048,3,64]{0,2,1:T(8,128)}, bf16[4,512,3,64]{1,3,2,0:T(8,128)(2,1)}, s32[4]{0:T(128)S(1)}, /*in...) while((s32[]{:T(128)}, f32[2048,3,64]{0,2,1:T(8,128)}, ...), condition=%wide.region_18.18_spmd.clone, body=%wide.region_16.17_spmd.clone.sunk | while | flops 2063661568 | bytes 143911376 | solution.py:103
  1176.6 144.6 %while.69 = (s32[]{:T(128)}, f32[2048,3,64]{0,2,1:T(8,128)}, f32[2048,3,64]{0,2,1:T(8,128)}, bf16[4,512,3,64]{1,3,2,0:T(8,128)(2,1)}, s32[4]{0:T(128)S(1)}, /*in...) while((s32[]{:T(128)}, f32[2048,3,64]{0,2,1:T(8,128)}, ...), condition=%wide.region_18.18_spmd.clone, body=%wide.region_16.17_spmd.clone.sunk | while | flops 2063661568 | bytes 143911376 | solution.py:103
  1350.6 12.1 add_convert_fusion
  1362.8 10.1 convolution_bitcast_fusion.1
  1372.9 12.4 convolution_bitcast_fusion
  1400.1 41.4 %all-reduce.15 = (f32[768]{0:T(1024)S(1)}, f32[768]{0:T(1024)S(1)}, f32[768]{0:T(1024)S(1)}, f32[768]{0:T(1024)S(1)}, f32[768]{0:T(1024)S(1)}, /*index=5*/f32[768]{0:T(1024)S(1)}) all-reduce(f32[768]{0:T(1024)S(1)} %copy-done.37, f32[768]{0:T(1024)S(1)} %copy-done.30, ...), channel_id=15, replica_groups=mesh['dp'=8,'tensor'=4] {'dp','tensor'}, use_global_device_ids=true, to_apply=%region_34.35.clone | all-reduce | flops 4608 | bytes 36864
  1460.0 37.4 %all-reduce.16 = (f32[3,64]{1,0:T(4,128)S(1)}, f32[3,64]{1,0:T(4,128)S(1)}, f32[12,64]{1,0:T(8,128)S(1)}) all-reduce(f32[3,64]{1,0:T(4,128)S(1)} %convert_reduce_fusion.1, f32[3,64]{1,0:T(4,128)S(1)} %convert_reduce_fusion.2, f32[12,64]{1,0:T(8,128)S(1)} %reshape.284), channel_id=10, replica_groups=mesh['dp'=8,'tensor'=4] {'dp'}, use_global_device_ids=true, to_apply=%region_26.27.clone | all-reduce | flops 1152 | bytes 9216
  1503.9 65.3 %reduce-scatter.32.cloned.1.call-done = f32[768,96]{0,1:T(8,128)} async-done(((f32[768,768]{0,1:T(8,128)}), f32[768,96]{0,1:T(8,128)}) %reduce-scatter.32.cloned.1.call-update) | async-done | bytes 294928 | tf_op jit(solution)/shard_map/reduce_scatter | solution.py:301
  1569.2 66.4 %reduce-scatter.34.cloned.1.call-done = f32[96,192]{1,0:T(8,128)} async-done(((f32[768,192]{1,0:T(8,128)}), f32[96,192]{1,0:T(8,128)}) %reduce-scatter.34.cloned.1.call-update) | async-done | bytes 73744
  1635.6 66.1 %reduce-scatter.36.cloned.1.call-done = f32[96,192]{1,0:T(8,128)} async-done(((f32[768,192]{1,0:T(8,128)}), f32[96,192]{1,0:T(8,128)}) %reduce-scatter.36.cloned.1.call-update) | async-done | bytes 73744
  1701.7 66.2 %reduce-scatter.38.cloned.1.call-done = f32[96,192]{1,0:T(8,128)} async-done(((f32[768,192]{1,0:T(8,128)}), f32[96,192]{1,0:T(8,128)}) %reduce-scatter.38.cloned.1.call-update) | async-done | bytes 73744
  (441 shorter events, 546.1 us)
Async XLA Ops:
  8.0 166.1 %all-gather.8.cloned.1.call-start = ((), (), s32[]{:S(2)}) async-start(), calls=%async_computation.10 | async-start | bytes 7864320 | tf_op jit(solution)/shard_map/all_gather | solution.py:167
  8.8 514.5 %reduce-scatter.22.cloned.1.call-start = ((), (), s32[]{:S(2)}) async-start(), calls=%async_computation.11 | async-start | bytes 15728640 | tf_op jit(solution)/shard_map/reduce_scatter | solution.py:190
  111.5 72.3 %copy-start.23 = (bf16[768,192]{1,0:T(8,128)(2,1)}, bf16[768,192]{1,0:T(8,128)(2,1)S(1)}, u32[]{:S(2)}) copy-start(bf16[768,192]{1,0:T(8,128)(2,1)S(1)} %all_gather.57) | copy-start | bytes 884740
  142.9 41.0 %copy-start.17 = (bf16[768,192]{1,0:T(8,128)(2,1)}, bf16[768,192]{1,0:T(8,128)(2,1)S(1)}, u32[]{:S(2)}) copy-start(bf16[768,192]{1,0:T(8,128)(2,1)S(1)} %all_gather.59) | copy-start | bytes 884740
  174.1 9.8 copy-start.19
  417.1 6.8 copy-start.13
  424.0 135.2 %all-gather.12.cloned.1.call-start = ((), (), s32[]{:S(2)}) async-start(), calls=%async_computation.13 | async-start | bytes 1327104 | tf_op jit(solution)/shard_map/all_gather | solution.py:152
  424.6 150.6 %all-gather.10.cloned.1.call-start = ((), (), s32[]{:S(2)}) async-start(), calls=%async_computation.12 | async-start | bytes 7864320 | tf_op jit(solution)/shard_map/all_gather | solution.py:194
  528.9 96.1 %all-gather.14.cloned.1.call-start = ((), (), s32[]{:S(2)}) async-start(), calls=%async_computation.14 | async-start | bytes 1327104 | tf_op jit(solution)/shard_map/all_gather | solution.py:153
  529.5 205.6 %reduce-scatter.24.cloned.1.call-start = ((), (), s32[]{:S(2)}) async-start(), calls=%async_computation.15 | async-start | bytes 15728640 | tf_op jit(solution)/shard_map/reduce_scatter | solution.py:205
  575.2 17.9 %copy-start.32 = (f32[768]{0:T(1024)S(1)}, f32[768]{0:T(1024)}, u32[]{:S(2)}) copy-start(f32[768]{0:T(1024)} %reshape.287) | copy-start | bytes 9220
  635.2 302.5 %reduce-scatter.26.cloned.1.call-start = ((), (), s32[]{:S(2)}) async-start(), calls=%async_computation.16 | async-start | bytes 15728640 | tf_op jit(solution)/shard_map/reduce_scatter | solution.py:243
  747.4 36.3 %collective-permute-start = (bf16[2,512,768]{2,1,0:T(8,128)(2,1)}, bf16[2,512,768]{2,1,0:T(8,128)(2,1)}, u32[]{:S(2)}, u32[]{:S(2)}) collective-permute-start(bf16[2,512,768]{2,1,0:T(8,128)(2,1)} %get-tuple-element.835), channel_id=1, source_target_pairs={{0,1},{1,2},{2,3},{3,0},{4,5},{5,6},{6,7},{7,4},{8,9},{9,10},{10,1... | collective-permute-start | bytes 4718600 | tf_op jit(solution)/shard_map/ppermute | solution.py:219
  747.4 46.3 %collective-permute-start.1 = (bf16[2,512,768]{2,1,0:T(8,128)(2,1)}, bf16[2,512,768]{2,1,0:T(8,128)(2,1)}, u32[]{:S(2)}, u32[]{:S(2)}) collective-permute-start(bf16[2,512,768]{2,1,0:T(8,128)(2,1)} %get-tuple-element.835), channel_id=1, source_target_pairs={{0,3},{1,0},{2,1},{3,2},{4,7},{5,4},{6,5},{7,6},{8,11},{9,8},{10,9... | collective-permute-start | bytes 4718600 | tf_op jit(solution)/shard_map/ppermute | solution.py:222
  783.8 20.2 %collective-permute-start.2 = (bf16[2,512,768]{2,1,0:T(8,128)(2,1)}, bf16[2,512,768]{2,1,0:T(8,128)(2,1)}, u32[]{:S(2)}, u32[]{:S(2)}) collective-permute-start(bf16[2,512,768]{2,1,0:T(8,128)(2,1)} %collective-permute-done), channel_id=1, source_target_pairs={{0,1},{1,2},{2,3},{3,0},{4,5},{5,6},{6,7},{7,4},{8,9},{9,10},{10,1... | collective-permute-start | bytes 4718600 | tf_op jit(solution)/shard_map/ppermute | solution.py:219
  809.3 18.0 %copy-start.39 = (bf16[768,768]{1,0:T(8,128)(2,1)S(1)}, bf16[768,768]{1,0:T(8,128)(2,1)}, u32[]{:S(2)}) copy-start(bf16[768,768]{1,0:T(8,128)(2,1)} %all-gather.12.cloned.1.call-done) | copy-start | bytes 3538948
  837.9 155.4 %all-gather.16.cloned.1.call-start = ((), (), s32[]{:S(2)}) async-start(), calls=%async_computation.17 | async-start | bytes 7864320 | tf_op jit(solution)/shard_map/all_gather | solution.py:249
  943.2 50.1 %copy-start.14 = (bf16[2,2048,192]{1,0,2:T(2,128)(2,1)S(1)}, bf16[2,2048,192]{1,0,2:T(2,128)(2,1)}, u32[]{:S(2)}) copy-start(bf16[2,2048,192]{1,0,2:T(2,128)(2,1)} %copy-done.13) | copy-start | bytes 4718596
  943.2 56.5 %copy-start.25 = (f32[2,512]{1,0:T(2,128)}, f32[2,512]{1,0:T(2,128)S(1)}, u32[]{:S(2)}) copy-start(f32[2,512]{1,0:T(2,128)S(1)} %negate_multiply_fusion.1) | copy-start | bytes 12292
  947.0 551.8 %reduce-scatter.40.cloned.1.call-start = ((), (), s32[]{:S(2)}) async-start(), calls=%async_computation.24 | async-start | bytes 884736
  999.8 500.7 %reduce-scatter.28.cloned.1.call-start = ((), (), s32[]{:S(2)}) async-start(), calls=%async_computation.18 | async-start | bytes 7864320 | tf_op jit(solution)/shard_map/reduce_scatter | solution.py:290
  1006.5 331.4 %copy-start.18 = (bf16[768,192]{1,0:T(8,128)(2,1)S(1)}, bf16[768,192]{1,0:T(8,128)(2,1)}, u32[]{:S(2)}) copy-start(bf16[768,192]{1,0:T(8,128)(2,1)} %copy-done.17) | copy-start | bytes 884740
  1013.9 7.9 copy-start.2
  1049.2 7.9 copy-start.2
  1085.7 7.9 copy-start.2
  1122.1 7.8 copy-start.2
  1158.5 7.2 copy-start.4
  1158.5 7.2 copy-start.10
  1176.6 7.9 copy-start.2
  1211.9 7.9 copy-start.2
  1248.4 7.9 copy-start.2
  1284.8 7.8 copy-start.2
  1321.2 7.1 copy-start.4
  1321.2 7.1 copy-start.10
  1362.7 141.2 %reduce-scatter.30.cloned.1.call-start = ((), (), s32[]{:S(2)}) async-start(), calls=%async_computation.19 | async-start | bytes 2654208 | tf_op jit(solution)/shard_map/reduce_scatter | solution.py:300
  1372.9 196.3 %reduce-scatter.32.cloned.1.call-start = ((), (), s32[]{:S(2)}) async-start(), calls=%async_computation.20 | async-start | bytes 2654208 | tf_op jit(solution)/shard_map/reduce_scatter | solution.py:301
  1385.4 250.3 %reduce-scatter.34.cloned.1.call-start = ((), (), s32[]{:S(2)}) async-start(), calls=%async_computation.21 | async-start | bytes 884736
  1392.7 7.3 copy-start.38
  1392.7 7.4 copy-start.30
  1392.7 7.4 copy-start.31
  1392.7 7.4 copy-start.34
  1392.8 7.3 copy-start.35
  1392.8 7.3 copy-start.36
  1392.8 7.3 copy-start.37
  1392.8 308.9 %reduce-scatter.36.cloned.1.call-start = ((), (), s32[]{:S(2)}) async-start(), calls=%async_computation.22 | async-start | bytes 884736
  1398.7 369.3 %reduce-scatter.38.cloned.1.call-start = ((), (), s32[]{:S(2)}) async-start(), calls=%async_computation.23 | async-start | bytes 884736
  1450.1 50.4 %copy-start.6 = (f32[2,512,768]{2,1,0:T(8,128)S(1)}, f32[2,512,768]{2,1,0:T(8,128)}, u32[]{:S(2)}) copy-start(f32[2,512,768]{2,1,0:T(8,128)} %copy-done.5) | copy-start | bytes 9437188
  1450.1 50.4 %copy-start.26 = (f32[2,512]{1,0:T(2,128)S(1)}, f32[2,512]{1,0:T(2,128)}, u32[]{:S(2)}) copy-start(f32[2,512]{1,0:T(2,128)} %copy-done.25) | copy-start | bytes 12292
  (48 other events, 178.6 us)
Sparse Core Ops, SparseCore 0:
  10.4 49.0 all-gather.7
  424.1 99.0 reduce-scatter.21
  838.0 99.6 reduce-scatter.25
Sparse Core Ops, SparseCore 1:
  426.7 40.1 all-gather.11
  529.0 46.2 all-gather.9
  577.3 41.4 all-gather.13
  635.3 99.7 reduce-scatter.23
  947.1 46.2 all-gather.15
  999.8 63.3 reduce-scatter.39
  1362.8 59.4 reduce-scatter.27
  1426.3 69.8 reduce-scatter.29
  1500.1 69.1 reduce-scatter.31
  1573.1 62.5 reduce-scatter.33
  1639.4 62.3 reduce-scatter.35
  1705.6 62.3 reduce-scatter.37
